TPU v7x, 32 devices: a whole 2x2x4 slice. The times are simulated.
32 devices in a mesh: pool: 2 (over core), ep: 4 (over z), half: 4 (over y, x).
Axes of the slice: x: 2, y: 2, z: 4, core: 2. Of those that a mesh axis runs over, the one named last changes fastest.
Arguments:
- tokens: bfloat16 [2, 256, 4096], P('pool', 'ep'), may hold values from -6 to 6
- routes: int32 [2, 256, 8], P('pool', 'ep'), may hold values from 0 to 31, all different within a row; in each aligned block of 64 rows (0 to 63, 64 to 127, ..., all dimensions but the last counted through in order) at most 32 rows name the same one
- router: bfloat16 [4096, 32], replicated, may hold values from -0.03125 to 0.03125
- w_gate: bfloat16 [32, 4096, 1536], P('ep', None, 'half'), may hold values from -0.09375 to 0.09375
- w_up: bfloat16 [32, 4096, 1536], P('ep', None, 'half'), may hold values from -0.09375 to 0.09375
- w_down: bfloat16 [32, 1536, 4096], P('ep', 'half'), may hold values from -0.625 to 0.625
- norm_gain: float32 [4096], replicated, may hold values from 0.1 to 1.9
- w_kv: bfloat16 [4096, 2048], P('ep', 'half'), may hold values from -0.09375 to 0.09375
- lengths: int32 [2, 4, 2], P(None, 'ep'), may hold values from 1 to 48, 64 in all within a row
- queries: bfloat16 [2, 1024, 2048], P('pool', 'ep', 'half'), may hold values from -150 to 150
- new_keys: bfloat16 [2, 1024, 1024], P('pool', 'ep', 'half'), may hold values from -5 to 5
- new_values: bfloat16 [2, 1024, 1024], P('pool', 'ep', 'half'), may hold values from -6 to 6
- w_out: bfloat16 [2048, 2048], P('half'), may hold values from -0.125 to 0.125
Outputs:
- decoded: bfloat16 [2, 1024, 2048], P('pool', ('ep', 'half'))
Inputs may be any that keep to these rules, and one draw needn't show every extreme that they name: `routes`: each token names 8 different experts; within each aligned block of 64 tokens no expert is named by more than 32 tokens. The 2 lengths of a group sum to 64.
All inputs are finite; a program needn't handle non-finite values.
Results may differ from a plain program's by a relative error of at most 0.022.
Values may be sent and summed in bfloat16 or wider, within the bound.
No kernel may reach another device: no remote copies, remote signals or barrier semaphores. Data moves between devices by JAX's collectives and lax.ppermute only.
A program may use at most 192 MiB of HBM per device.

v0:
```python
import math

import jax
import jax.numpy as jnp
from jax import lax
from jax.sharding import PartitionSpec as P

HEAD = 128
SAMPLES = 128
CAP = 32


def from_partner(shard, axis, stride):
    return lax.ppermute(shard, axis, [(i, i ^ 1 << stride) for i in range(lax.axis_size(axis))])


def expand(form, rows, w_gate, w_up):
    gate = jnp.einsum(form, rows, w_gate, preferred_element_type=jnp.float32)
    up = jnp.einsum(form, rows, w_up, preferred_element_type=jnp.float32)
    return (jax.nn.silu(gate) * up).astype(jnp.bfloat16)


def attend(block, prompt_lengths, query, fresh_key, fresh_value):
    group_tok = block.shape[0]
    group_rows = query.shape[0]
    ends = jnp.cumsum(prompt_lengths)
    position = jnp.arange(group_tok, dtype=jnp.int32)
    segment = jnp.sum((position[:, None] >= ends[None, :]).astype(jnp.int32), axis=1)
    prompt = jnp.arange(group_rows, dtype=jnp.int32) // SAMPLES
    allowed = segment[None, :] == prompt[:, None]
    keys = block[:, :, 0, :]
    values = block[:, :, 1, :]
    scale = 1.0 / math.sqrt(HEAD)
    scores = jnp.einsum("rhgd,thd->rhgt", query, keys, preferred_element_type=jnp.float32) * scale
    scores = jnp.where(allowed[:, None, None, :], scores, -1e30)
    own = jnp.einsum("rhgd,rhd->rhg", query, fresh_key, preferred_element_type=jnp.float32) * scale
    top = jnp.maximum(jnp.max(scores, axis=3), own)
    spread = jnp.where(allowed[:, None, None, :], jnp.exp(scores - top[..., None]), 0.0)
    self_weight = jnp.exp(own - top)
    total = jnp.sum(spread, axis=3) + self_weight
    probs = (spread / total[..., None]).astype(jnp.bfloat16)
    self_prob = (self_weight / total).astype(jnp.bfloat16)
    mixed = jnp.einsum("rhgt,thd->rhgd", probs, values, preferred_element_type=jnp.float32)
    mixed = (
        mixed
        + self_prob.astype(jnp.float32)[..., None] * fresh_value.astype(jnp.float32)[:, :, None, :]
    )
    return mixed.astype(jnp.bfloat16).reshape(group_rows, -1)


def on_device(
    tokens,
    routes,
    router,
    w_gate,
    w_up,
    w_down,
    norm_gain,
    w_kv,
    lengths,
    queries,
    new_keys,
    new_values,
    w_out,
):
    inputs = tokens[0]
    chosen = routes[0]
    experts = router.shape[1]
    local_experts = w_gate.shape[0]
    model = inputs.shape[1]
    ep_count = lax.axis_size("ep")
    half_count = lax.axis_size("half")
    part_slots = CAP // half_count
    feature_rows = model // half_count
    logits = jnp.dot(inputs, router, preferred_element_type=jnp.float32)
    picked = jnp.take_along_axis(logits, chosen, axis=1)
    weights = jax.nn.softmax(picked, axis=1).reshape(-1)
    flat = chosen.reshape(-1)
    onehot = (flat[:, None] == jnp.arange(experts, dtype=jnp.int32)[None, :]).astype(jnp.int32)
    before = jnp.cumsum(onehot, axis=0) - onehot
    rank = jnp.sum(before * onehot, axis=1)
    slot = flat * CAP + rank
    select = (slot[:, None] == jnp.arange(experts * CAP, dtype=jnp.int32)[None, :]).astype(
        jnp.bfloat16
    )
    select = jnp.sum(select.reshape(inputs.shape[0], -1, experts * CAP), axis=1)
    outgoing = jnp.einsum("ts,td->sd", select, inputs, preferred_element_type=jnp.float32).astype(
        jnp.bfloat16
    )
    outgoing = outgoing.reshape(ep_count, local_experts, CAP, model)
    mine = outgoing.reshape(ep_count, local_experts, half_count, part_slots, model)
    mine = lax.dynamic_index_in_dim(mine, lax.axis_index("half"), 2, keepdims=False)
    received = lax.all_to_all(mine, "ep", split_axis=0, concat_axis=0, tiled=True)
    pieces = expand(
        "qsecd,edf->qsecf", lax.all_gather(received[None], "half", axis=0, tiled=True), w_gate, w_up
    )
    hidden = jnp.transpose(pieces, (2, 1, 0, 3, 4))
    hidden = hidden.reshape(local_experts, ep_count * CAP, -1)
    columns = w_down
    summed = lax.psum_scatter(
        jnp.einsum("erf,efd->der", hidden, columns, preferred_element_type=jnp.float32).astype(
            jnp.bfloat16
        ),
        "half",
        scatter_dimension=0,
        tiled=True,
    ).astype(jnp.float32)
    summed = summed.astype(jnp.bfloat16).reshape(feature_rows, local_experts, ep_count, CAP)
    back = lax.all_to_all(summed, "ep", split_axis=2, concat_axis=2, tiled=True)
    flat_back = back.reshape(feature_rows, -1)
    column = flat % local_experts * (ep_count * CAP) + flat // local_experts * CAP + rank
    arrived = flat_back[:, column].astype(jnp.float32)
    weighted = jnp.sum(
        (arrived * weights[None, :]).reshape(feature_rows, inputs.shape[0], -1), axis=2
    )
    moe_whole = lax.all_gather(weighted.T.astype(jnp.bfloat16), "half", axis=1, tiled=True).astype(
        jnp.float32
    )
    mixed = inputs.astype(jnp.float32) + moe_whole
    meansq = jnp.mean(mixed * mixed, axis=1, keepdims=True)
    normed = (mixed * lax.rsqrt(meansq + 1e-06) * norm_gain).astype(jnp.bfloat16)
    columns = normed
    keyvals = jnp.dot(
        columns, lax.all_gather(w_kv, "ep", axis=0, tiled=True), preferred_element_type=jnp.float32
    ).astype(jnp.bfloat16)
    remote = from_partner(keyvals, "pool", 0)
    other = 1 - lax.axis_index("pool")
    prompt_lengths = lax.dynamic_index_in_dim(lengths, other, 0, keepdims=False)[0]
    kv_heads = new_keys.shape[2] // HEAD
    block = remote.reshape(remote.shape[0], kv_heads, 2, HEAD)
    query = queries[0].reshape(queries.shape[1], kv_heads, -1, HEAD)
    fresh_key = new_keys[0].reshape(new_keys.shape[1], kv_heads, HEAD)
    fresh_value = new_values[0].reshape(new_values.shape[1], kv_heads, HEAD)
    attention = attend(block, prompt_lengths, query, fresh_key, fresh_value)
    decoded = lax.psum_scatter(
        jnp.dot(attention, w_out, preferred_element_type=jnp.float32).astype(jnp.bfloat16),
        "half",
        scatter_dimension=0,
        tiled=True,
    )
    return decoded[None]


def solution(mesh):
    in_specs = (
        P("pool", "ep", None),
        P("pool", "ep", None),
        P(),
        P("ep", None, "half"),
        P("ep", None, "half"),
        P("ep", "half", None),
        P(),
        P("ep", "half"),
        P(None, "ep", None),
        P("pool", "ep", "half"),
        P("pool", "ep", "half"),
        P("pool", "ep", "half"),
        P("half", None),
    )
    out_specs = P("pool", ("ep", "half"), None)
    return jax.shard_map(
        on_device, mesh=mesh, in_specs=in_specs, out_specs=out_specs, check_vma=False
    )
```

profile of v0, /device:TPU:0, one launch (start us, length us, event | category | flops | bytes accessed | tf_op | source)
XLA Modules:
  0.0 415.9 jit_solution(12743380232631339659)
XLA Ops:
  7.4 0.9 copy.48
  8.5 1.2 reduce-window.18
  10.1 0.7 fusion.18
  10.8 6.6 %convolution_convert_fusion = bf16[1024,4096]{1,0:T(8,128)(2,1)} fusion(bf16[64,1024]{1,0:T(8,128)(2,1)S(1)} %fusion.18, bf16[1,64,4096]{2,1,0:T(8,128)(2,1)} %param.13), kind=kOutput, calls=%fused_computation.7 | convolution fusion | flops 541065216 | bytes 9043968 | tf_op jit(solution)/shard_map/ts,td->sd/dot_general | solution.py:87
  17.5 1.7 dynamic-slice_bitcast_fusion
  19.2 54.5 %all_to_all.10 = bf16[4,8,8,4096]{3,2,1,0:T(8,128)(2,1)} all-to-all(bf16[4,8,8,4096]{3,2,1,0:T(8,128)(2,1)S(1)} %dynamic-slice_bitcast_fusion), channel_id=1, replica_groups=mesh['pool'=2,'ep'=4,'half'=4] {'ep'}, dimensions={0} | all-to-all | bytes 4194304 | tf_op jit(solution)/shard_map/all_to_all | solution.py:93
  73.9 86.6 %all-gather.6.cloned.1.call-done = bf16[16,8,8,4096]{3,2,1,0:T(8,128)(2,1)} async-done(((bf16[4,8,8,4096]{3,2,1,0:T(8,128)(2,1)}), bf16[16,8,8,4096]{3,2,1,0:T(8,128)(2,1)}) %all-gather.6.cloned.1.call-update) | async-done | bytes 8388624 | tf_op jit(solution)/shard_map/all_gather | solution.py:95
  160.6 7.7 %copy.53 = bf16[16,8,8,4096]{3,2,0,1:T(8,128)(2,1)} copy(bf16[16,8,8,4096]{3,2,1,0:T(8,128)(2,1)} %all-gather.6.cloned.1.call-done) | data formatting | bytes 16777216 | tf_op jit(solution)/shard_map/all_gather | solution.py:95
  168.3 13.0 %bitcast_multiply_fusion.2 = f32[8,4,4,8,384]{4,3,1,2,0:T(8,128)S(1)} fusion(bf16[4,4,8,8,4096]{4,3,1,0,2:T(8,128)(2,1)} %bitcast.154, bf16[8,4096,384]{2,1,0:T(8,128)(2,1)} %param.16), kind=kOutput, calls=%fused_computation.16 | convolution fusion | flops 3222798336 | bytes 35127296 | tf_op jit(solution)/shard_map/qsecd,edf->qsecf/dot_general | solution.py:18
  181.3 13.2 %fusion.6 = bf16[8,4,4,8,384]{4,3,1,2,0:T(8,128)(2,1)S(1)} fusion(f32[8,4,4,8,384]{4,3,1,2,0:T(8,128)S(1)} %bitcast_multiply_fusion.2, bf16[4,4,8,8,4096]{4,3,1,0,2:T(8,128)(2,1)} %bitcast.155, bf16[8,4096,384]{2,1,0:T(8,128)(2,1)} %param.17), kind=kOutput, calls=%fused_computation.15 | convolution fusion | flops 3222011904 | bytes 35913728 | tf_op jit(solution)/shard_map/qsecd,edf->qsecf/dot_general | solution.py:19
  194.6 15.9 %convert_bitcast_fusion = bf16[4096,8,128]{0,2,1:T(8,128)(2,1)} fusion(bf16[8,128,384]{2,1,0:T(8,128)(2,1)S(1)} %bitcast.158, bf16[8,384,4096]{2,1,0:T(8,128)(2,1)} %param.18), kind=kOutput, calls=%fused_computation.6 | convolution fusion | flops 3225419776 | bytes 34340864 | tf_op jit(solution)/shard_map/erf,efd->der/dot_general | solution.py:101
  210.5 0.5 all-gather.4.cloned.1.call-update
  211.1 85.9 %reduce-scatter.3.cloned.1.call-done = bf16[1024,8,128]{0,2,1:T(8,128)(2,1)} async-done(((bf16[4096,8,128]{0,2,1:T(8,128)(2,1)}), bf16[1024,8,128]{0,2,1:T(8,128)(2,1)}) %reduce-scatter.3.cloned.1.call-update) | async-done | bytes 2097168 | tf_op jit(solution)/shard_map/reduce_scatter | solution.py:100
  297.0 3.2 copy.55
  300.2 4.6 %all-to-all-start.1 = ((bf16[1024,8,4,32]{0,3,1,2:T(8,128)(2,1)}), bf16[1024,8,4,32]{0,3,1,2:T(8,128)(2,1)}, u32[]{:S(2)}, u32[]{:S(2)}) async-start(bf16[1024,8,4,32]{0,3,1,2:T(8,128)(2,1)} %copy.55), calls=%async_computation.2 | async-start | bytes 4194304 | tf_op jit(solution)/shard_map/all_to_all | solution.py:109
  305.2 0.3 fusion.20
  305.5 3.9 gather_fusion.1
  309.7 1.0 reshape_squeeze.14
  310.7 0.8 reshape.363
  312.0 2.3 fusion.52
  314.4 38.7 %all-to-all-done.1 = bf16[1024,8,4,32]{0,3,1,2:T(8,128)(2,1)} async-done(((bf16[1024,8,4,32]{0,3,1,2:T(8,128)(2,1)}), bf16[1024,8,4,32]{0,3,1,2:T(8,128)(2,1)}, u32[]{:S(2)}, u32[]{:S(2)}) %all-to-all-start.1) | async-done | bytes 2097184 | tf_op jit(solution)/shard_map/all_to_all | solution.py:109
  353.0 3.2 copy.56
  356.2 5.4 %gather_fusion = bf16[512,1024]{1,0:T(8,128)(2,1)} fusion(bf16[1024,1024]{0,1:T(8,128)(2,1)} %bitcast.156, s32[1024]{0:T(1024)S(1)} %pad_clamp_fusion), kind=kCustom, calls=%fused_computation | custom fusion | bytes 2099200 | tf_op jit(solution)/shard_map/gather | solution.py:112
  361.6 1.9 fusion.4
  363.5 10.6 %all_gather.10 = bf16[64,4096]{1,0:T(8,128)(2,1)S(1)} all-gather(bf16[64,1024]{1,0:T(8,128)(2,1)S(1)} %bitcast.160), channel_id=1, replica_groups=mesh['pool'=2,'ep'=4,'half'=4] {'half'}, dimensions={1}, use_global_device_ids=true | all-gather | bytes 655360 | tf_op jit(solution)/shard_map/all_gather | solution.py:116
  374.1 0.3 multiply_reduce_fusion
  374.4 3.1 convolution_convert_fusion.2
  377.7 1.1 copy.67
  378.8 1.0 copy.69
  380.3 0.3 fusion.15
  380.6 1.7 convolution_convert_fusion.1
  382.3 26.4 %reduce-scatter.5.cloned.1.call-done = bf16[64,2048]{1,0:T(8,128)(2,1)} async-done(((bf16[256,2048]{1,0:T(8,128)(2,1)}), bf16[64,2048]{1,0:T(8,128)(2,1)}) %reduce-scatter.5.cloned.1.call-update) | async-done | bytes 262160 | tf_op jit(solution)/shard_map/reduce_scatter | solution.py:135
  (56 shorter events, 2.9 us)
Async XLA Ops:
  7.4 373.2 %copy-start = (bf16[512,2048]{1,0:T(8,128)(2,1)S(1)}, bf16[512,2048]{1,0:T(8,128)(2,1)}, u32[]{:S(2)}) copy-start(bf16[512,2048]{1,0:T(8,128)(2,1)} %param.25) | copy-start | bytes 6291460
  7.4 153.2 %all-gather.6.cloned.1.call-start = ((), (), s32[]{:S(2)}) async-start(), calls=%async_computation.7 | async-start | bytes 10485760 | tf_op jit(solution)/shard_map/all_gather | solution.py:95
  73.7 223.3 %reduce-scatter.3.cloned.1.call-start = ((), (), s32[]{:S(2)}) async-start(), calls=%async_computation.4 | async-start | bytes 10485760 | tf_op jit(solution)/shard_map/reduce_scatter | solution.py:100
  210.5 163.9 %all-gather.4.cloned.1.call-start = ((), (), s32[]{:S(2)}) async-start(), calls=%async_computation.5 | async-start | bytes 5242880 | tf_op jit(solution)/shard_map/all_gather | solution.py:124
  297.0 8.1 %copy-start.5 = (s32[1,64,8]{1,2,0:T(8,128)S(1)}, s32[1,64,8]{1,2,0:T(8,128)}, u32[]{:S(2)}) copy-start(s32[1,64,8]{1,2,0:T(8,128)} %param.14) | copy-start | bytes 6148
  297.0 8.2 %copy-start.1 = (bf16[1,64,4096]{2,1,0:T(8,128)(2,1)S(1)}, bf16[1,64,4096]{2,1,0:T(8,128)(2,1)}, u32[]{:S(2)}) copy-start(bf16[1,64,4096]{2,1,0:T(8,128)(2,1)} %param.13) | copy-start | bytes 1572868
  297.0 8.3 %copy-start.2 = (bf16[4096,32]{0,1:T(8,128)(2,1)S(1)}, bf16[4096,32]{0,1:T(8,128)(2,1)}, u32[]{:S(2)}) copy-start(bf16[4096,32]{0,1:T(8,128)(2,1)} %param.15) | copy-start | bytes 786436
  300.2 52.8 %all-to-all-start.1 = ((bf16[1024,8,4,32]{0,3,1,2:T(8,128)(2,1)}), bf16[1024,8,4,32]{0,3,1,2:T(8,128)(2,1)}, u32[]{:S(2)}, u32[]{:S(2)}) async-start(bf16[1024,8,4,32]{0,3,1,2:T(8,128)(2,1)} %copy.55), calls=%async_computation.2 | async-start | bytes 4194304 | tf_op jit(solution)/shard_map/all_to_all | solution.py:109
  304.8 103.9 %reduce-scatter.5.cloned.1.call-start = ((), (), s32[]{:S(2)}) async-start(), calls=%async_computation.6 | async-start | bytes 1310720 | tf_op jit(solution)/shard_map/reduce_scatter | solution.py:135
  305.5 4.0 copy-start.6
  305.5 5.2 %copy-start.3 = (bf16[1,256,256]{2,1,0:T(8,128)(2,1)S(1)}, bf16[1,256,256]{2,1,0:T(8,128)(2,1)}, u32[]{:S(2)}) copy-start(bf16[1,256,256]{2,1,0:T(8,128)(2,1)} %param.23) | copy-start | bytes 393220
  356.2 18.3 %copy-start.4 = (f32[4096]{0:T(1024)S(1)}, f32[4096]{0:T(1024)}, u32[]{:S(2)}) copy-start(f32[4096]{0:T(1024)} %param.19) | copy-start | bytes 49156
  377.6 2.2 collective-permute-start
Sparse Core Ops, SparseCore 0:
  73.8 86.7 all-gather.5
  210.6 86.3 reduce-scatter.2
  382.4 26.2 reduce-scatter.4
Sparse Core Ops, SparseCore 1:
  212.5 80.6 all-gather.3
where the time goes:
time: 417 us; the launch traced here: 416 us
  waiting for transfers between devices  238 us (57%)
  blocking collectives  65.1 us (16%)
  matrix products  56.6 us (14%)
  local copies, waits for them, and re-layouts  30.9 us (7%)
  between operations  14.9 us (4%)
  other arithmetic  5.1 us (1%)
  starting transfers between devices  5.05 us (1%)
    all_gather x1, waiting for transfers between devices, on_device(): lax.all_gather(received[None], 'half', axis=0, tiled=True)  86.6 us
    reduce_scatter x1, waiting for transfers between devices, on_device(): lax.psum_scatter(jnp.einsum('erf,efd->der', hidden, columns, preferred_el...  85.9 us
    all_to_all x1, blocking collectives, on_device(): lax.all_to_all(mine, 'ep', split_axis=0, concat_axis=0, tiled=True)  54.5 us
    all_to_all x1, waiting for transfers between devices, on_device(): back = lax.all_to_all(summed, 'ep', split_axis=2, concat_axis=2, tiled=True)  38.7 us
    reduce_scatter x1, waiting for transfers between devices, on_device(): lax.psum_scatter(jnp.dot(attention, w_out, preferred_element_type=jnp.flo...  26.4 us
    dot_general x1, matrix products, on_device(): jnp.einsum('erf,efd->der', hidden, columns, preferred_element_type=jnp.fl...  15.9 us
    dot_general x1, matrix products, expand(): up = jnp.einsum(form, rows, w_up, preferred_element_type=jnp.float32)  13.2 us
    dot_general x1, matrix products, expand(): gate = jnp.einsum(form, rows, w_gate, preferred_element_type=jnp.float32)  13 us
  transfers between devices with their start and end apart: 6, of which 4 were waited for; matrix products, arithmetic and copies ran while one was open for 6% of the time, Pallas kernels for 0%

commit v1 on v0

v1 whole, which is shorter than its diff:
```python
import functools
import math

import jax
import jax.numpy as jnp
from jax import lax
from jax.experimental import pallas as pl
from jax.experimental.pallas import tpu as pltpu
from jax.sharding import PartitionSpec as P

HEAD = 128
SAMPLES = 128
LANES = 128
F32 = jnp.float32
BF16 = jnp.bfloat16
WHOLE = pl.BlockSpec(memory_space=pltpu.VMEM)


def swap(shard, axis, bits):
    return lax.ppermute(shard, axis, [(i, i ^ bits) for i in range(lax.axis_size(axis))])


def shift(shard, axis, distance):
    count = lax.axis_size(axis)
    return lax.ppermute(shard, axis, [(i, (i + distance) % count) for i in range(count)])


def params(steps):
    return pltpu.CompilerParams(
        dimension_semantics=("arbitrary",) * steps, vmem_limit_bytes=60 * 1024 * 1024
    )


def columns_of(piece, width):
    return pl.ds(pl.multiple_of(piece * width, width), width)


def expand_kernel(parts, top, place, own, *refs):
    others, refs = refs[:parts], refs[parts:]
    tags, router, refs = refs[0], refs[1], refs[2:]
    gates, ups, refs = refs[:parts], refs[parts : 2 * parts], refs[2 * parts :]
    hidden, rows, weights = refs
    half, first = place[0], place[1]
    local, width = own.shape[0], rows.shape[2]
    step = pl.program_id(0)

    @pl.when(step == 0)
    def _():
        logits = jnp.zeros(weights.shape, F32)
        for k in range(parts):
            columns = columns_of(half ^ k, width)
            rows[k, :local, :] = own[:, columns]
            rows[k, local:, :] = others[k][...]
            logits += lax.dot_general(
                rows[k], router[:, columns], (((1,), (1,)), ((), ())), preferred_element_type=F32
            )
        expert = lax.broadcasted_iota(jnp.int32, weights.shape, 1)
        named = tags[...].astype(F32).astype(jnp.int32)
        picked = named[:, 0:1] == expert
        for j in range(1, top):
            picked = jnp.logical_or(picked, named[:, j : j + 1] == expert)
        most = jnp.max(jnp.where(picked, logits, -1e30), axis=1, keepdims=True)
        spread = jnp.where(picked, jnp.exp(logits - most), 0.0)
        weights[...] = spread / jnp.sum(spread, axis=1, keepdims=True)

    gate = jnp.zeros(hidden.shape, F32)
    up = jnp.zeros(hidden.shape, F32)
    for k in range(parts):
        gate += jnp.dot(rows[k], gates[k][0], preferred_element_type=F32)
        up += jnp.dot(rows[k], ups[k][0], preferred_element_type=F32)
    expert = lax.broadcasted_iota(jnp.int32, weights.shape, 1)
    scale = jnp.sum(
        jnp.where(expert == first + step, weights[...], 0.0), axis=1, keepdims=True
    )
    hidden[...] = (gate / (1.0 + jnp.exp(-gate)) * up * scale).astype(BF16)


def expand(place, own, others, tags, router, w_gate, w_up, top):
    parts = len(others)
    local, model = own.shape
    tokens = tags.shape[0]
    experts, units = w_gate.shape[0], w_gate.shape[2]
    width = model // parts
    weight = [
        pl.BlockSpec((1, width, units), lambda e, place, k=k: (e, place[0] ^ k, 0))
        for k in range(parts)
    ]
    return pl.pallas_call(
        functools.partial(expand_kernel, parts, top),
        out_shape=jax.ShapeDtypeStruct((tokens, experts * units), BF16),
        grid_spec=pltpu.PrefetchScalarGridSpec(
            num_scalar_prefetch=1,
            grid=(experts,),
            in_specs=[WHOLE] * (parts + 3) + weight + weight,
            out_specs=pl.BlockSpec((tokens, units), lambda e, place: (0, e)),
            scratch_shapes=[
                pltpu.VMEM((parts, tokens, width), BF16),
                pltpu.VMEM((tokens, router.shape[0]), F32),
            ],
        ),
        compiler_params=params(1),
        name="expand",
    )(place, own, *others, tags, router, *[w_gate] * parts, *[w_up] * parts)


def reduce_kernel(place, hidden, w_down, out):
    weight = w_down[...].reshape(-1, w_down.shape[2])
    out[...] = jnp.dot(hidden[...], weight, preferred_element_type=F32).astype(BF16)


def reduce(piece, hidden, w_down, width, block):
    experts, units, model = w_down.shape
    steps = width // block
    return pl.pallas_call(
        reduce_kernel,
        out_shape=jax.ShapeDtypeStruct((hidden.shape[0], width), BF16),
        grid_spec=pltpu.PrefetchScalarGridSpec(
            num_scalar_prefetch=1,
            grid=(steps,),
            in_specs=[
                WHOLE,
                pl.BlockSpec(
                    (experts, units, block), lambda i, piece: (0, 0, piece[0] * steps + i)
                ),
            ],
            out_specs=pl.BlockSpec((hidden.shape[0], block), lambda i, piece: (0, i)),
        ),
        compiler_params=params(1),
        name="reduce",
    )(piece, hidden, w_down)


def project_kernel(parts, eps, place, own, *refs):
    moe, refs = refs[:parts], refs[parts:]
    gain, home, refs = refs[0], refs[1], refs[2:]
    mine, theirs, out, mixed, normed = refs
    half, ep, pool = place[0], place[1], place[2]
    width = moe[0].shape[1]
    square = jnp.zeros((own.shape[0], 1), F32)
    for k in range(parts):
        columns = columns_of(half ^ k, width)
        value = own[:, columns].astype(F32) + moe[k][...].astype(F32)
        mixed[:, columns] = value
        square += jnp.sum(value * value, axis=1, keepdims=True)
    factor = lax.rsqrt(square / mixed.shape[1] + 1e-06)
    normed[...] = (mixed[...] * factor * gain[...]).astype(BF16)
    depth, narrow = home.shape[0], mine.shape[1]
    for side, pieces in ((pool, mine), (1 - pool, theirs)):
        kept = columns_of(side, narrow)
        total = jnp.dot(
            normed[:, columns_of(ep, depth)], home[:, kept], preferred_element_type=F32
        )
        for d in range(1, eps):
            origin = lax.rem(ep + eps - d, eps)
            total += jnp.dot(
                normed[:, columns_of(origin, depth)],
                pieces[(d - 1) * depth : d * depth, :],
                preferred_element_type=F32,
            )
        out[:, kept] = total.astype(BF16)


def project(place, own, moe, gain, home, mine, theirs, eps):
    return pl.pallas_call(
        functools.partial(project_kernel, len(moe), eps),
        out_shape=jax.ShapeDtypeStruct((own.shape[0], home.shape[1]), BF16),
        grid_spec=pltpu.PrefetchScalarGridSpec(
            num_scalar_prefetch=1,
            grid=(),
            in_specs=[WHOLE] * (len(moe) + 5),
            out_specs=WHOLE,
            scratch_shapes=[pltpu.VMEM(own.shape, F32), pltpu.VMEM(own.shape, BF16)],
        ),
        compiler_params=params(0),
        name="project",
    )(place, own, *moe, gain, home, mine, theirs)


def attend_kernel(prompts, place, block, query, fresh_key, fresh_value, w_out, out):
    rows = query.shape[0]
    group_tok = block.shape[0]
    kv_heads = fresh_key.shape[1] // HEAD
    per_head = query.shape[1] // HEAD // kv_heads
    position = lax.broadcasted_iota(jnp.int32, (rows, group_tok), 1)
    row = place[0] * rows + lax.broadcasted_iota(jnp.int32, (rows, group_tok), 0)
    segment = jnp.zeros((rows, group_tok), jnp.int32)
    end = jnp.int32(0)
    for p in range(prompts):
        end = end + place[1 + p]
        segment += (position >= end).astype(jnp.int32)
    allowed = segment == row // SAMPLES
    scale = 1.0 / math.sqrt(HEAD)
    heads = []
    for kv in range(kv_heads):
        key = block[:, 2 * kv * HEAD : (2 * kv + 1) * HEAD]
        value = block[:, (2 * kv + 1) * HEAD : (2 * kv + 2) * HEAD]
        new_key = fresh_key[:, kv * HEAD : (kv + 1) * HEAD].astype(F32)
        new_value = fresh_value[:, kv * HEAD : (kv + 1) * HEAD].astype(F32)
        for j in range(per_head):
            head = (kv * per_head + j) * HEAD
            asked = query[:, head : head + HEAD]
            scores = (
                lax.dot_general(asked, key, (((1,), (1,)), ((), ())), preferred_element_type=F32)
                * scale
            )
            scores = jnp.where(allowed, scores, -1e30)
            own = jnp.sum(asked.astype(F32) * new_key, axis=1, keepdims=True) * scale
            top = jnp.maximum(jnp.max(scores, axis=1, keepdims=True), own)
            spread = jnp.where(allowed, jnp.exp(scores - top), 0.0)
            self_weight = jnp.exp(own - top)
            total = jnp.sum(spread, axis=1, keepdims=True) + self_weight
            probs = (spread / total).astype(BF16)
            self_prob = (self_weight / total).astype(BF16).astype(F32)
            mixed = jnp.dot(probs, value, preferred_element_type=F32) + self_prob * new_value
            heads.append(mixed.astype(BF16))
    attention = jnp.concatenate(heads, axis=1)
    out[...] = jnp.dot(attention, w_out[...], preferred_element_type=F32).astype(BF16)


def attend(piece, prompt_lengths, block, query, fresh_key, fresh_value, w_out, rows):
    prompts = prompt_lengths.shape[0]

    def cut(array):
        return pl.BlockSpec((rows, array.shape[1]), lambda i, place: (place[0], 0))

    return pl.pallas_call(
        functools.partial(attend_kernel, prompts),
        out_shape=jax.ShapeDtypeStruct((rows, w_out.shape[1]), BF16),
        grid_spec=pltpu.PrefetchScalarGridSpec(
            num_scalar_prefetch=1,
            grid=(1,),
            in_specs=[WHOLE, cut(query), cut(fresh_key), cut(fresh_value), WHOLE],
            out_specs=pl.BlockSpec((rows, w_out.shape[1]), lambda i, place: (0, 0)),
        ),
        compiler_params=params(1),
        name="attend",
    )(
        jnp.concatenate([piece, prompt_lengths]),
        block,
        query,
        fresh_key,
        fresh_value,
        w_out,
    )


def total_of(first, rest):
    value = first.astype(F32)
    for other in rest:
        value = value + other.astype(F32)
    return value


def on_device(
    tokens,
    routes,
    router,
    w_gate,
    w_up,
    w_down,
    norm_gain,
    w_kv,
    lengths,
    queries,
    new_keys,
    new_values,
    w_out,
):
    own = tokens[0]
    chosen = routes[0]
    local, model = own.shape
    top = chosen.shape[1]
    eps = lax.axis_size("ep")
    parts = lax.axis_size("half")
    half, ep, pool = lax.axis_index("half"), lax.axis_index("ep"), lax.axis_index("pool")
    width = model // parts

    tags = jnp.pad(chosen.astype(BF16), ((0, 0), (0, LANES - top)))
    quarter = lax.dynamic_slice_in_dim(own, half * width, width, axis=1)
    parcel = jnp.concatenate([quarter, tags], axis=1)
    arrived = [shift(parcel, "ep", d) for d in range(1, eps)]
    near = jnp.concatenate([a[:, :width] for a in arrived], axis=0)
    all_tags = jnp.concatenate([tags] + [a[:, width:] for a in arrived], axis=0)
    order = sorted(range(1, parts), key=lambda k: -bin(k).count("1"))
    others = [near] + [None] * (parts - 1)
    for k in order:
        others[k] = swap(near, "half", k)

    narrow = w_kv.shape[1] // 2
    piece, near = lax.optimization_barrier(
        (lax.dynamic_slice_in_dim(w_kv, pool * narrow, narrow, axis=1), near)
    )
    others[0] = near
    mine = jnp.concatenate([shift(piece, "ep", d) for d in range(1, eps)], axis=0)
    theirs = swap(mine, "pool", 1)

    place = jnp.stack([half, ep * w_gate.shape[0]])
    hidden = expand(place, own, others, all_tags, router.T, w_gate, w_up, top)
    partial = [None] * parts
    for k in order + [0]:
        partial[k] = reduce((half ^ k)[None], hidden, w_down, width, 256)
    gathered = [swap(partial[k], "half", k) for k in order]
    summed = total_of(partial[0], gathered)
    returned = [
        shift(summed[d * local : (d + 1) * local].astype(BF16), "ep", -d) for d in range(1, eps)
    ]
    moe_quarter = total_of(summed[:local], returned).astype(BF16)
    moe = [moe_quarter] + [None] * (parts - 1)
    for k in order:
        moe[k] = swap(moe_quarter, "half", k)
    keyvals = project(
        jnp.stack([half, ep, pool]), own, moe, norm_gain[None], w_kv, mine, theirs, eps
    )
    block = swap(keyvals, "pool", 1)

    prompt_lengths = lax.dynamic_index_in_dim(lengths, 1 - pool, 0, keepdims=False)[0]
    rows = queries.shape[1] // parts
    decoded = [None] * parts
    for k in order + [0]:
        decoded[k] = attend(
            (half ^ k)[None],
            prompt_lengths,
            block,
            queries[0],
            new_keys[0],
            new_values[0],
            w_out,
            rows,
        )
    sent = [swap(decoded[k], "half", k) for k in order]
    return total_of(decoded[0], sent).astype(BF16)[None]


def solution(mesh):
    in_specs = (
        P("pool", "ep", None),
        P("pool", "ep", None),
        P(),
        P("ep", None, "half"),
        P("ep", None, "half"),
        P("ep", "half", None),
        P(),
        P("ep", "half"),
        P(None, "ep", None),
        P("pool", "ep", "half"),
        P("pool", "ep", "half"),
        P("pool", "ep", "half"),
        P("half", None),
    )
    out_specs = P("pool", ("ep", "half"), None)
    return jax.shard_map(
        on_device, mesh=mesh, in_specs=in_specs, out_specs=out_specs, check_vma=False
    )
```

time: 417 us -> 174 us (0.42)
  waiting for transfers between devices: 238 us -> 57.3 us
  Pallas kernels: 0 us -> 75.7 us
  blocking collectives: 65.1 us -> 0 us
  matrix products: 56.6 us -> 0 us
  local copies, waits for them, and re-layouts: 30.9 us -> 6.69 us
  starting transfers between devices: 5.05 us -> 26.9 us
  between operations: 14.9 us -> 0.22 us
    reduce_scatter x2 -> x0, waiting for transfers between devices: 112 us -> none  [the longest x1 85.9 us: on_device(): lax.psum_scatter(jnp.einsum('erf,efd->der', hidden, columns, preferred_el...]
    all_gather x2 -> x0, waiting for transfers between devices: 86.7 us -> none  [the longest x1 86.6 us: on_device(): lax.all_gather(received[None], 'half', axis=0, tiled=True)]
    pallas_call x0 -> x10, Pallas kernels: none -> 75.7 us  [the longest x1 27.2 us: expand(): pl.pallas_call(functools.partial(expand_kernel, parts, top), out_shape=ja...]
    ppermute x1 -> x23, waiting for transfers between devices: 0.01 us -> 57.3 us  [the longest x14 35.9 us: swap(): lax.ppermute(shard, axis, [(i, i ^ bits) for i in range(lax.axis_size(axi...]
    dot_general x10 -> x0, matrix products: 56.6 us -> none  [the longest x1 15.9 us: on_device(): jnp.einsum('erf,efd->der', hidden, columns, preferred_element_type=jnp.fl...]
    all_to_all x1 -> x0, blocking collectives: 54.5 us -> none  [on_device(): lax.all_to_all(mine, 'ep', split_axis=0, concat_axis=0, tiled=True)]
    all_to_all x1 -> x0, waiting for transfers between devices: 38.7 us -> none  [on_device(): back = lax.all_to_all(summed, 'ep', split_axis=2, concat_axis=2, tiled=True)]
    ppermute x1 -> x23, starting transfers between devices: 0.07 us -> 26.9 us  [the longest x14 14.2 us: swap(): lax.ppermute(shard, axis, [(i, i ^ bits) for i in range(lax.axis_size(axi...]
  transfers between devices with their start and end apart: 6 -> 23, of which waited for: 4 -> 15; matrix products, arithmetic and copies ran while one was open for 6% -> 3% of each run, Pallas kernels for 0% -> 38%
where the time goes in v1:
time: 174 us; the launch traced here: 173 us
  Pallas kernels  75.7 us (44%)
  waiting for transfers between devices  57.3 us (33%)
  starting transfers between devices  26.9 us (15%)
  local copies, waits for them, and re-layouts  6.69 us (4%)
  other arithmetic  6.2 us (4%)
    ppermute x14, waiting for transfers between devices, swap(): lax.ppermute(shard, axis, [(i, i ^ bits) for i in range(lax.axis_size(axi...  35.9 us
    pallas_call x1, Pallas kernels, expand(): pl.pallas_call(functools.partial(expand_kernel, parts, top), out_shape=ja...  27.2 us
    pallas_call x4, Pallas kernels, reduce(): pl.pallas_call(reduce_kernel, out_shape=jax.ShapeDtypeStruct((hidden.shap...  24.2 us
    ppermute x9, waiting for transfers between devices, shift(): lax.ppermute(shard, axis, [(i, (i + distance) % count) for i in range(cou...  21.4 us
    pallas_call x4, Pallas kernels, attend(): pl.pallas_call(functools.partial(attend_kernel, prompts), out_shape=jax.S...  19.4 us
    ppermute x14, starting transfers between devices, swap(): lax.ppermute(shard, axis, [(i, i ^ bits) for i in range(lax.axis_size(axi...  14.2 us
    ppermute x9, starting transfers between devices, shift(): lax.ppermute(shard, axis, [(i, (i + distance) % count) for i in range(cou...  12.8 us
    pallas_call x1, Pallas kernels, project(): pl.pallas_call(functools.partial(project_kernel, len(moe), eps), out_shap...  5.01 us
  transfers between devices with their start and end apart: 23, of which 15 were waited for; matrix products, arithmetic and copies ran while one was open for 3% of the time, Pallas kernels for 38%

profile of v1, /device:TPU:0, one launch (start us, length us, event | category | flops | bytes accessed | tf_op | source)
XLA Modules:
  0.0 173.1 jit_solution(15398548235254575129)
XLA Ops:
  1.8 5.1 %collective-permute-start.2 = (bf16[64,1152]{1,0:T(8,128)(2,1)S(1)}, bf16[64,1152]{1,0:T(8,128)(2,1)S(1)}, u32[]{:S(2)}, u32[]{:S(2)}) collective-permute-start(bf16[64,1152]{1,0:T(8,128)(2,1)S(1)} %pad_maximum_fusion.1), channel_id=1, source_target_pairs={{0,12},{4,0},{8,4},{12,8},{1,13},{5,1},{9,5},{13,9},{2,14},{6,2},{... | collective-permute-start | bytes 442376 | tf_op jit(solution)/shard_map/ppermute | solution.py:25
  8.0 3.3 %collective-permute-done.2 = bf16[64,1152]{1,0:T(8,128)(2,1)S(1)} collective-permute-done((bf16[64,1152]{1,0:T(8,128)(2,1)S(1)}, bf16[64,1152]{1,0:T(8,128)(2,1)S(1)}, u32[]{:S(2)}, u32[]{:S(2)}) %collective-permute-start.2) | collective-permute-done | bytes 147488 | tf_op jit(solution)/shard_map/ppermute | solution.py:25
  11.3 8.2 %collective-permute-done.1 = bf16[64,1152]{1,0:T(8,128)(2,1)S(1)} collective-permute-done((bf16[64,1152]{1,0:T(8,128)(2,1)S(1)}, bf16[64,1152]{1,0:T(8,128)(2,1)S(1)}, u32[]{:S(2)}, u32[]{:S(2)}) %collective-permute-start.1) | collective-permute-done | bytes 147488 | tf_op jit(solution)/shard_map/ppermute | solution.py:25
  20.9 2.5 %collective-permute-start.5 = (bf16[192,1024]{1,0:T(8,128)(2,1)S(1)}, bf16[192,1024]{1,0:T(8,128)(2,1)S(1)}, u32[]{:S(2)}, u32[]{:S(2)}) collective-permute-start(bf16[192,1024]{1,0:T(8,128)(2,1)S(1)} %pad_maximum_fusion.refs_0_), channel_id=1, source_target_pairs={{0,3},{1,2},{2,1},{3,0},{4,7},{5,6},{6,5},{7,4},{8,11},{9,10},{10,... | collective-permute-start | bytes 1179656 | tf_op jit(solution)/shard_map/ppermute | solution.py:20
  24.4 1.9 %collective-permute-start.16 = (bf16[1024,256]{1,0:T(8,128)(2,1)}, bf16[1024,256]{1,0:T(8,128)(2,1)S(1)}, u32[]{:S(2)}, u32[]{:S(2)}) collective-permute-start(bf16[1024,256]{1,0:T(8,128)(2,1)} %constant_dynamic-slice_fusion), channel_id=1, source_target_pairs={{0,8},{4,12},{8,0},{12,4},{1,9},{5,13},{9,1},{13,5},{2,10},{6,14},... | collective-permute-start | bytes 1572872 | tf_op jit(solution)/shard_map/ppermute | solution.py:25
  27.4 6.5 %collective-permute-done.5.refs_3_ = bf16[192,1024]{1,0:T(8,128)(2,1)S(1)} collective-permute-done((bf16[192,1024]{1,0:T(8,128)(2,1)S(1)}, bf16[192,1024]{1,0:T(8,128)(2,1)S(1)}, u32[]{:S(2)}, u32[]{:S(2)}) %collective-permute-start.5) | collective-permute-done | bytes 393248 | tf_op jit(solution)/shard_map/ppermute | solution.py:20
  35.5 5.2 %collective-permute-done.4.refs_2_ = bf16[192,1024]{1,0:T(8,128)(2,1)S(1)} collective-permute-done((bf16[192,1024]{1,0:T(8,128)(2,1)S(1)}, bf16[192,1024]{1,0:T(8,128)(2,1)S(1)}, u32[]{:S(2)}, u32[]{:S(2)}) %collective-permute-start.4) | collective-permute-done | bytes 393248 | tf_op jit(solution)/shard_map/ppermute | solution.py:20
  41.6 27.2 %expand.1.hidden = bf16[256,3072]{1,0:T(8,128)(2,1)} custom-call(s32[2]{0:T(128)} %pad_add_fusion.1.place, bf16[64,4096]{1,0:T(8,128)(2,1)} %bitcast.25, bf16[192,1024]{1,0:T(8,128)(2,1)} %copy-done.4, bf16[192,1024]{1,0:T(8,128)(2,1)} %copy-done.9, bf16[192,1024]{1,0:T(8,128)(2,1)} %copy-done.8, bf16[192,1024]{1,0:T(8,128)(2,1)} %copy-done.7, ...), custom_call_target="tpu_custom_call" | custom-call | tf_op jit(solution)/shard_map/expand/pallas_call | solution.py:88
  68.8 5.9 %reduce.7 = bf16[256,1024]{1,0:T(8,128)(2,1)} custom-call(s32[1]{0:T(128)} %bitcast.11.place, bf16[256,3072]{1,0:T(8,128)(2,1)} %expand.1.hidden, bf16[8,384,4096]{2,1,0:T(8,128)(2,1)} %w_down.7), custom_call_target="tpu_custom_call" | custom-call | tf_op jit(solution)/shard_map/reduce/pallas_call | solution.py:114
  74.7 5.9 %reduce.6 = bf16[256,1024]{1,0:T(8,128)(2,1)} custom-call(s32[1]{0:T(128)} %bitcast.10.place, bf16[256,3072]{1,0:T(8,128)(2,1)} %expand.1.hidden, bf16[8,384,4096]{2,1,0:T(8,128)(2,1)} %w_down.7), custom_call_target="tpu_custom_call" | custom-call | tf_op jit(solution)/shard_map/reduce/pallas_call | solution.py:114
  80.6 6.0 %reduce.5 = bf16[256,1024]{1,0:T(8,128)(2,1)} custom-call(s32[1]{0:T(128)} %bitcast.9.place, bf16[256,3072]{1,0:T(8,128)(2,1)} %expand.1.hidden, bf16[8,384,4096]{2,1,0:T(8,128)(2,1)} %w_down.7), custom_call_target="tpu_custom_call" | custom-call | tf_op jit(solution)/shard_map/reduce/pallas_call | solution.py:114
  86.5 2.4 %collective-permute-start.6 = (bf16[256,1024]{1,0:T(8,128)(2,1)}, bf16[256,1024]{1,0:T(8,128)(2,1)S(1)}, u32[]{:S(2)}, u32[]{:S(2)}) collective-permute-start(bf16[256,1024]{1,0:T(8,128)(2,1)} %reduce.5), channel_id=1, source_target_pairs={{0,3},{1,2},{2,1},{3,0},{4,7},{5,6},{6,5},{7,4},{8,11},{9,10},{10,... | collective-permute-start | bytes 1572872 | tf_op jit(solution)/shard_map/ppermute | solution.py:20
  90.3 6.4 %reduce.4 = bf16[256,1024]{1,0:T(8,128)(2,1)} custom-call(s32[1]{0:T(128)} %bitcast.place, bf16[256,3072]{1,0:T(8,128)(2,1)} %expand.1.hidden, bf16[8,384,4096]{2,1,0:T(8,128)(2,1)} %w_down.7), custom_call_target="tpu_custom_call" | custom-call | tf_op jit(solution)/shard_map/reduce/pallas_call | solution.py:114
  96.7 5.8 %collective-permute-done.6 = bf16[256,1024]{1,0:T(8,128)(2,1)S(1)} collective-permute-done((bf16[256,1024]{1,0:T(8,128)(2,1)}, bf16[256,1024]{1,0:T(8,128)(2,1)S(1)}, u32[]{:S(2)}, u32[]{:S(2)}) %collective-permute-start.6) | collective-permute-done | bytes 524320 | tf_op jit(solution)/shard_map/ppermute | solution.py:20
  102.5 10.4 %collective-permute-done.7 = bf16[256,1024]{1,0:T(8,128)(2,1)} collective-permute-done((bf16[256,1024]{1,0:T(8,128)(2,1)}, bf16[256,1024]{1,0:T(8,128)(2,1)}, u32[]{:S(2)}, u32[]{:S(2)}) %collective-permute-start.7) | collective-permute-done | bytes 524320 | tf_op jit(solution)/shard_map/ppermute | solution.py:20
  112.9 1.7 fusion.5
  114.8 2.0 %collective-permute-start.11 = (bf16[64,1024]{1,0:T(8,128)(2,1)S(1)}, bf16[64,1024]{1,0:T(8,128)(2,1)S(1)}, u32[]{:S(2)}, u32[]{:S(2)}) collective-permute-start(bf16[64,1024]{1,0:T(8,128)(2,1)S(1)} %get-tuple-element.12), channel_id=1, source_target_pairs={{0,4},{4,8},{8,12},{12,0},{1,5},{5,9},{9,13},{13,1},{2,6},{6,10},{... | collective-permute-start | bytes 393224 | tf_op jit(solution)/shard_map/ppermute | solution.py:25
  116.8 2.0 %collective-permute-start.10 = (bf16[64,1024]{1,0:T(8,128)(2,1)S(1)}, bf16[64,1024]{1,0:T(8,128)(2,1)S(1)}, u32[]{:S(2)}, u32[]{:S(2)}) collective-permute-start(bf16[64,1024]{1,0:T(8,128)(2,1)S(1)} %get-tuple-element.13), channel_id=1, source_target_pairs={{0,8},{4,12},{8,0},{12,4},{1,9},{5,13},{9,1},{13,5},{2,10},{6,14},... | collective-permute-start | bytes 393224 | tf_op jit(solution)/shard_map/ppermute | solution.py:25
  118.8 1.7 collective-permute-done.9
  120.5 5.0 %collective-permute-done.11 = bf16[64,1024]{1,0:T(8,128)(2,1)S(1)} collective-permute-done((bf16[64,1024]{1,0:T(8,128)(2,1)S(1)}, bf16[64,1024]{1,0:T(8,128)(2,1)S(1)}, u32[]{:S(2)}, u32[]{:S(2)}) %collective-permute-start.11) | collective-permute-done | bytes 131104 | tf_op jit(solution)/shard_map/ppermute | solution.py:25
  125.5 3.3 %collective-permute-done.10 = bf16[64,1024]{1,0:T(8,128)(2,1)S(1)} collective-permute-done((bf16[64,1024]{1,0:T(8,128)(2,1)S(1)}, bf16[64,1024]{1,0:T(8,128)(2,1)S(1)}, u32[]{:S(2)}, u32[]{:S(2)}) %collective-permute-start.10) | collective-permute-done | bytes 131104 | tf_op jit(solution)/shard_map/ppermute | solution.py:25
  128.8 2.5 %collective-permute-start.14 = (bf16[64,1024]{1,0:T(8,128)(2,1)S(1)}, bf16[64,1024]{1,0:T(8,128)(2,1)S(1)}, u32[]{:S(2)}, u32[]{:S(2)}) collective-permute-start(bf16[64,1024]{1,0:T(8,128)(2,1)S(1)} %fusion.3.refs_0_), channel_id=1, source_target_pairs={{0,3},{1,2},{2,1},{3,0},{4,7},{5,6},{6,5},{7,4},{8,11},{9,10},{10,... | collective-permute-start | bytes 393224 | tf_op jit(solution)/shard_map/ppermute | solution.py:20
  133.0 2.2 %collective-permute-done.14.refs_3_ = bf16[64,1024]{1,0:T(8,128)(2,1)S(1)} collective-permute-done((bf16[64,1024]{1,0:T(8,128)(2,1)S(1)}, bf16[64,1024]{1,0:T(8,128)(2,1)S(1)}, u32[]{:S(2)}, u32[]{:S(2)}) %collective-permute-start.14) | collective-permute-done | bytes 131104 | tf_op jit(solution)/shard_map/ppermute | solution.py:20
  135.2 2.2 %collective-permute-done.13.refs_2_ = bf16[64,1024]{1,0:T(8,128)(2,1)S(1)} collective-permute-done((bf16[64,1024]{1,0:T(8,128)(2,1)S(1)}, bf16[64,1024]{1,0:T(8,128)(2,1)S(1)}, u32[]{:S(2)}, u32[]{:S(2)}) %collective-permute-start.13) | collective-permute-done | bytes 131104 | tf_op jit(solution)/shard_map/ppermute | solution.py:20
  138.8 5.0 %project.1 = bf16[64,512]{1,0:T(8,128)(2,1)} custom-call(s32[3]{0:T(128)} %pad_add_fusion.place, bf16[64,4096]{1,0:T(8,128)(2,1)} %bitcast.26, bf16[64,1024]{1,0:T(8,128)(2,1)} %copy-done.6, bf16[64,1024]{1,0:T(8,128)(2,1)} %collective-permute-done.12.refs_1_, bf16[64,1024]{1,0:T(8,128)(2,1)} %copy-done.14, bf16[64,1024]{1,0:T(8,128)(2,1)} %copy-done.13, ...), custom_call_target="tpu_custom_call" | custom-call | tf_op jit(solution)/shard_map/project/pallas_call | solution.py:164
  145.9 4.8 %attend.5 = bf16[64,2048]{1,0:T(8,128)(2,1)} custom-call(s32[3]{0:T(128)} %get-tuple-element.15.place, bf16[64,512]{1,0:T(8,128)(2,1)} %copy-done.5, bf16[256,512]{1,0:T(8,128)(2,1)} %bitcast.21, bf16[256,256]{1,0:T(8,128)(2,1)} %bitcast.27, bf16[256,256]{1,0:T(8,128)(2,1)} %bitcast.31, bf16[512,2048]{1,0:T(8,128)(2,1)} %w_out.7), custom_call_target="tpu_custom_call" | custom-call | tf_op jit(solution)/shard_map/attend/pallas_call | solution.py:226
  150.7 1.6 collective-permute-start.20
  152.3 4.8 %attend.6 = bf16[64,2048]{1,0:T(8,128)(2,1)} custom-call(s32[3]{0:T(128)} %get-tuple-element.16.place, bf16[64,512]{1,0:T(8,128)(2,1)} %copy-done.5, bf16[256,512]{1,0:T(8,128)(2,1)} %bitcast.22, bf16[256,256]{1,0:T(8,128)(2,1)} %bitcast.28, bf16[256,256]{1,0:T(8,128)(2,1)} %bitcast.32, bf16[512,2048]{1,0:T(8,128)(2,1)} %w_out.7), custom_call_target="tpu_custom_call" | custom-call | tf_op jit(solution)/shard_map/attend/pallas_call | solution.py:226
  158.4 4.8 %attend.7 = bf16[64,2048]{1,0:T(8,128)(2,1)} custom-call(s32[3]{0:T(128)} %get-tuple-element.17.place, bf16[64,512]{1,0:T(8,128)(2,1)} %copy-done.5, bf16[256,512]{1,0:T(8,128)(2,1)} %bitcast.23, bf16[256,256]{1,0:T(8,128)(2,1)} %bitcast.29, bf16[256,256]{1,0:T(8,128)(2,1)} %bitcast.33, bf16[512,2048]{1,0:T(8,128)(2,1)} %w_out.7), custom_call_target="tpu_custom_call" | custom-call | tf_op jit(solution)/shard_map/attend/pallas_call | solution.py:226
  163.9 4.8 %attend.4 = bf16[64,2048]{1,0:T(8,128)(2,1)} custom-call(s32[3]{0:T(128)} %get-tuple-element.14.place, bf16[64,512]{1,0:T(8,128)(2,1)} %copy-done.5, bf16[256,512]{1,0:T(8,128)(2,1)} %bitcast.24, bf16[256,256]{1,0:T(8,128)(2,1)} %bitcast.30, bf16[256,256]{1,0:T(8,128)(2,1)} %bitcast.34, bf16[512,2048]{1,0:T(8,128)(2,1)} %w_out.7), custom_call_target="tpu_custom_call" | custom-call | tf_op jit(solution)/shard_map/attend/pallas_call | solution.py:226
  168.8 2.5 %collective-permute-done.22 = bf16[64,2048]{1,0:T(8,128)(2,1)S(1)} collective-permute-done((bf16[64,2048]{1,0:T(8,128)(2,1)}, bf16[64,2048]{1,0:T(8,128)(2,1)S(1)}, u32[]{:S(2)}, u32[]{:S(2)}) %collective-permute-start.22) | collective-permute-done | bytes 262176 | tf_op jit(solution)/shard_map/ppermute | solution.py:20
  171.3 1.8 %fusion = bf16[1,64,2048]{2,1,0:T(8,128)(2,1)} fusion(bf16[64,2048]{1,0:T(8,128)(2,1)S(1)} %collective-permute-done.22, bf16[64,2048]{1,0:T(8,128)(2,1)S(1)} %collective-permute-done.21, bf16[64,2048]{1,0:T(8,128)(2,1)S(1)} %collective-permute-done.20, bf16[64,2048]{1,0:T(8,128)(2,1)} %attend.4), kind=kLoop, calls=%fused_computation.3 | loop fusion | flops 1048576 | bytes 1310720 | tf_op jit(solution)/shard_map/broadcast_in_dim | solution.py:331
  (82 shorter events, 17.3 us)
Async XLA Ops:
  0.0 133.0 %copy-start = (s32[2,1,2]{2,1,0:T(1,128)S(1)}, s32[2,1,2]{2,1,0:T(1,128)}, u32[]{:S(2)}) copy-start(s32[2,1,2]{2,1,0:T(1,128)} %param.21) | copy-start | bytes 52
  0.0 23.4 %copy-start.2 = (bf16[1024,512]{1,0:T(8,128)(2,1)S(1)}, bf16[1024,512]{1,0:T(8,128)(2,1)}, u32[]{:S(2)}) copy-start(bf16[1024,512]{1,0:T(8,128)(2,1)} %refs_5_.1) | copy-start | bytes 3145732
  1.8 9.4 %collective-permute-start.2 = (bf16[64,1152]{1,0:T(8,128)(2,1)S(1)}, bf16[64,1152]{1,0:T(8,128)(2,1)S(1)}, u32[]{:S(2)}, u32[]{:S(2)}) collective-permute-start(bf16[64,1152]{1,0:T(8,128)(2,1)S(1)} %pad_maximum_fusion.1), channel_id=1, source_target_pairs={{0,12},{4,0},{8,4},{12,8},{1,13},{5,1},{9,5},{13,9},{2,14},{6,2},{... | collective-permute-start | bytes 442376 | tf_op jit(solution)/shard_map/ppermute | solution.py:25
  7.0 12.5 %collective-permute-start.1 = (bf16[64,1152]{1,0:T(8,128)(2,1)S(1)}, bf16[64,1152]{1,0:T(8,128)(2,1)S(1)}, u32[]{:S(2)}, u32[]{:S(2)}) collective-permute-start(bf16[64,1152]{1,0:T(8,128)(2,1)S(1)} %pad_maximum_fusion.1), channel_id=1, source_target_pairs={{0,8},{4,12},{8,0},{12,4},{1,9},{5,13},{9,1},{13,5},{2,10},{6,14},... | collective-permute-start | bytes 442376 | tf_op jit(solution)/shard_map/ppermute | solution.py:25
  7.0 12.5 %collective-permute-start = (bf16[64,1152]{1,0:T(8,128)(2,1)S(1)}, bf16[64,1152]{1,0:T(8,128)(2,1)S(1)}, u32[]{:S(2)}, u32[]{:S(2)}) collective-permute-start(bf16[64,1152]{1,0:T(8,128)(2,1)S(1)} %pad_maximum_fusion.1), channel_id=1, source_target_pairs={{0,4},{4,8},{8,12},{12,0},{1,5},{5,9},{9,13},{13,1},{2,6},{6,10},{... | collective-permute-start | bytes 442376 | tf_op jit(solution)/shard_map/ppermute | solution.py:25
  11.2 8.2 %copy-start.10 = (bf16[64,1152]{1,0:T(8,128)(2,1)}, bf16[64,1152]{1,0:T(8,128)(2,1)S(1)}, u32[]{:S(2)}) copy-start(bf16[64,1152]{1,0:T(8,128)(2,1)S(1)} %collective-permute-done.2) | copy-start | bytes 442372
  20.8 14.1 %slice-start = ((bf16[64,1152]{1,0:T(8,128)(2,1)}), bf16[64,128]{1,0:T(8,128)(2,1)S(1)}, s32[]{:S(2)}) async-start(bf16[64,1152]{1,0:T(8,128)(2,1)} %copy-done.10), calls=%async_computation | async-start | bytes 32768 | tf_op jit(solution)/shard_map/slice | solution.py:283
  20.8 14.1 %slice-start.1 = ((bf16[64,1152]{1,0:T(8,128)(2,1)}), bf16[64,128]{1,0:T(8,128)(2,1)S(1)}, s32[]{:S(2)}) async-start(bf16[64,1152]{1,0:T(8,128)(2,1)} %copy-done.11), calls=%async_computation.1 | async-start | bytes 32768 | tf_op jit(solution)/shard_map/slice | solution.py:283
  20.8 14.1 %slice-start.2 = ((bf16[64,1152]{1,0:T(8,128)(2,1)}), bf16[64,128]{1,0:T(8,128)(2,1)S(1)}, s32[]{:S(2)}) async-start(bf16[64,1152]{1,0:T(8,128)(2,1)} %copy-done.12), calls=%async_computation.2 | async-start | bytes 32768 | tf_op jit(solution)/shard_map/slice | solution.py:283
  20.9 20.0 %copy-start.4 = (bf16[192,1024]{1,0:T(8,128)(2,1)}, bf16[192,1024]{1,0:T(8,128)(2,1)S(1)}, u32[]{:S(2)}) copy-start(bf16[192,1024]{1,0:T(8,128)(2,1)S(1)} %pad_maximum_fusion.refs_0_) | copy-start | bytes 1179652
  20.9 13.0 %collective-permute-start.5 = (bf16[192,1024]{1,0:T(8,128)(2,1)S(1)}, bf16[192,1024]{1,0:T(8,128)(2,1)S(1)}, u32[]{:S(2)}, u32[]{:S(2)}) collective-permute-start(bf16[192,1024]{1,0:T(8,128)(2,1)S(1)} %pad_maximum_fusion.refs_0_), channel_id=1, source_target_pairs={{0,3},{1,2},{2,1},{3,0},{4,7},{5,6},{6,5},{7,4},{8,11},{9,10},{10,... | collective-permute-start | bytes 1179656 | tf_op jit(solution)/shard_map/ppermute | solution.py:20
  24.2 65.3 %collective-permute-start.15 = (bf16[1024,256]{1,0:T(8,128)(2,1)}, bf16[1024,256]{1,0:T(8,128)(2,1)S(1)}, u32[]{:S(2)}, u32[]{:S(2)}) collective-permute-start(bf16[1024,256]{1,0:T(8,128)(2,1)} %constant_dynamic-slice_fusion), channel_id=1, source_target_pairs={{0,4},{4,8},{8,12},{12,0},{1,5},{5,9},{9,13},{13,1},{2,6},{6,10},{... | collective-permute-start | bytes 1572872 | tf_op jit(solution)/shard_map/ppermute | solution.py:25
  24.4 65.6 %collective-permute-start.16 = (bf16[1024,256]{1,0:T(8,128)(2,1)}, bf16[1024,256]{1,0:T(8,128)(2,1)S(1)}, u32[]{:S(2)}, u32[]{:S(2)}) collective-permute-start(bf16[1024,256]{1,0:T(8,128)(2,1)} %constant_dynamic-slice_fusion), channel_id=1, source_target_pairs={{0,8},{4,12},{8,0},{12,4},{1,9},{5,13},{9,1},{13,5},{2,10},{6,14},... | collective-permute-start | bytes 1572872 | tf_op jit(solution)/shard_map/ppermute | solution.py:25
  26.4 14.4 %collective-permute-start.4 = (bf16[192,1024]{1,0:T(8,128)(2,1)S(1)}, bf16[192,1024]{1,0:T(8,128)(2,1)S(1)}, u32[]{:S(2)}, u32[]{:S(2)}) collective-permute-start(bf16[192,1024]{1,0:T(8,128)(2,1)S(1)} %pad_maximum_fusion.refs_0_), channel_id=1, source_target_pairs={{0,2},{1,3},{2,0},{3,1},{4,6},{5,7},{6,4},{7,5},{8,10},{9,11},{10,... | collective-permute-start | bytes 1179656 | tf_op jit(solution)/shard_map/ppermute | solution.py:20
  26.9 13.9 %collective-permute-start.3 = (bf16[192,1024]{1,0:T(8,128)(2,1)S(1)}, bf16[192,1024]{1,0:T(8,128)(2,1)S(1)}, u32[]{:S(2)}, u32[]{:S(2)}) collective-permute-start(bf16[192,1024]{1,0:T(8,128)(2,1)S(1)} %pad_maximum_fusion.refs_0_), channel_id=1, source_target_pairs={{0,1},{1,0},{2,3},{3,2},{4,5},{5,4},{6,7},{7,6},{8,9},{9,8},{10,11... | collective-permute-start | bytes 1179656 | tf_op jit(solution)/shard_map/ppermute | solution.py:20
  33.9 7.0 %copy-start.7 = (bf16[192,1024]{1,0:T(8,128)(2,1)}, bf16[192,1024]{1,0:T(8,128)(2,1)S(1)}, u32[]{:S(2)}) copy-start(bf16[192,1024]{1,0:T(8,128)(2,1)S(1)} %collective-permute-done.5.refs_3_) | copy-start | bytes 1179652
  33.9 56.3 %collective-permute-start.17 = (bf16[1024,256]{1,0:T(8,128)(2,1)}, bf16[1024,256]{1,0:T(8,128)(2,1)S(1)}, u32[]{:S(2)}, u32[]{:S(2)}) collective-permute-start(bf16[1024,256]{1,0:T(8,128)(2,1)} %constant_dynamic-slice_fusion), channel_id=1, source_target_pairs={{0,12},{4,0},{8,4},{12,8},{1,13},{5,1},{9,5},{13,9},{2,14},{6,2},{... | collective-permute-start | bytes 1572872 | tf_op jit(solution)/shard_map/ppermute | solution.py:25
  86.5 15.9 %collective-permute-start.6 = (bf16[256,1024]{1,0:T(8,128)(2,1)}, bf16[256,1024]{1,0:T(8,128)(2,1)S(1)}, u32[]{:S(2)}, u32[]{:S(2)}) collective-permute-start(bf16[256,1024]{1,0:T(8,128)(2,1)} %reduce.5), channel_id=1, source_target_pairs={{0,3},{1,2},{2,1},{3,0},{4,7},{5,6},{6,5},{7,4},{8,11},{9,10},{10,... | collective-permute-start | bytes 1572872 | tf_op jit(solution)/shard_map/ppermute | solution.py:20
  89.0 23.9 %collective-permute-start.7 = (bf16[256,1024]{1,0:T(8,128)(2,1)}, bf16[256,1024]{1,0:T(8,128)(2,1)}, u32[]{:S(2)}, u32[]{:S(2)}) collective-permute-start(bf16[256,1024]{1,0:T(8,128)(2,1)} %reduce.6), channel_id=1, source_target_pairs={{0,1},{1,0},{2,3},{3,2},{4,5},{5,4},{6,7},{7,6},{8,9},{9,8},{10,11... | collective-permute-start | bytes 1572872 | tf_op jit(solution)/shard_map/ppermute | solution.py:20
  89.5 23.4 %collective-permute-start.8 = (bf16[256,1024]{1,0:T(8,128)(2,1)}, bf16[256,1024]{1,0:T(8,128)(2,1)}, u32[]{:S(2)}, u32[]{:S(2)}) collective-permute-start(bf16[256,1024]{1,0:T(8,128)(2,1)} %reduce.7), channel_id=1, source_target_pairs={{0,2},{1,3},{2,0},{3,1},{4,6},{5,7},{6,4},{7,5},{8,10},{9,11},{10,... | collective-permute-start | bytes 1572872 | tf_op jit(solution)/shard_map/ppermute | solution.py:20
  90.2 47.4 %collective-permute-start.18 = (bf16[3072,256]{1,0:T(8,128)(2,1)S(1)}, bf16[3072,256]{1,0:T(8,128)(2,1)S(1)}, u32[]{:S(2)}, u32[]{:S(2)}) collective-permute-start(bf16[3072,256]{1,0:T(8,128)(2,1)S(1)} %constant_dynamic-update-slice_fusion.refs_6_), channel_id=1, source_target_pairs={{0,16},{16,0},{1,17},{17,1},{2,18},{18,2},{3,19},{19,3},{4,20},{20... | collective-permute-start | bytes 4718600 | tf_op jit(solution)/shard_map/ppermute | solution.py:20
  114.7 5.8 %collective-permute-start.9 = (bf16[64,1024]{1,0:T(8,128)(2,1)S(1)}, bf16[64,1024]{1,0:T(8,128)(2,1)S(1)}, u32[]{:S(2)}, u32[]{:S(2)}) collective-permute-start(bf16[64,1024]{1,0:T(8,128)(2,1)S(1)} %get-tuple-element.11), channel_id=1, source_target_pairs={{0,12},{4,0},{8,4},{12,8},{1,13},{5,1},{9,5},{13,9},{2,14},{6,2},{... | collective-permute-start | bytes 393224 | tf_op jit(solution)/shard_map/ppermute | solution.py:25
  114.8 10.7 %collective-permute-start.11 = (bf16[64,1024]{1,0:T(8,128)(2,1)S(1)}, bf16[64,1024]{1,0:T(8,128)(2,1)S(1)}, u32[]{:S(2)}, u32[]{:S(2)}) collective-permute-start(bf16[64,1024]{1,0:T(8,128)(2,1)S(1)} %get-tuple-element.12), channel_id=1, source_target_pairs={{0,4},{4,8},{8,12},{12,0},{1,5},{5,9},{9,13},{13,1},{2,6},{6,10},{... | collective-permute-start | bytes 393224 | tf_op jit(solution)/shard_map/ppermute | solution.py:25
  116.8 12.0 %collective-permute-start.10 = (bf16[64,1024]{1,0:T(8,128)(2,1)S(1)}, bf16[64,1024]{1,0:T(8,128)(2,1)S(1)}, u32[]{:S(2)}, u32[]{:S(2)}) collective-permute-start(bf16[64,1024]{1,0:T(8,128)(2,1)S(1)} %get-tuple-element.13), channel_id=1, source_target_pairs={{0,8},{4,12},{8,0},{12,4},{1,9},{5,13},{9,1},{13,5},{2,10},{6,14},... | collective-permute-start | bytes 393224 | tf_op jit(solution)/shard_map/ppermute | solution.py:25
  128.8 8.8 %copy-start.6 = (bf16[64,1024]{1,0:T(8,128)(2,1)}, bf16[64,1024]{1,0:T(8,128)(2,1)S(1)}, u32[]{:S(2)}) copy-start(bf16[64,1024]{1,0:T(8,128)(2,1)S(1)} %fusion.3.refs_0_) | copy-start | bytes 393220
  128.8 6.4 %collective-permute-start.14 = (bf16[64,1024]{1,0:T(8,128)(2,1)S(1)}, bf16[64,1024]{1,0:T(8,128)(2,1)S(1)}, u32[]{:S(2)}, u32[]{:S(2)}) collective-permute-start(bf16[64,1024]{1,0:T(8,128)(2,1)S(1)} %fusion.3.refs_0_), channel_id=1, source_target_pairs={{0,3},{1,2},{2,1},{3,0},{4,7},{5,6},{6,5},{7,4},{8,11},{9,10},{10,... | collective-permute-start | bytes 393224 | tf_op jit(solution)/shard_map/ppermute | solution.py:20
  131.3 6.1 %collective-permute-start.13 = (bf16[64,1024]{1,0:T(8,128)(2,1)S(1)}, bf16[64,1024]{1,0:T(8,128)(2,1)S(1)}, u32[]{:S(2)}, u32[]{:S(2)}) collective-permute-start(bf16[64,1024]{1,0:T(8,128)(2,1)S(1)} %fusion.3.refs_0_), channel_id=1, source_target_pairs={{0,2},{1,3},{2,0},{3,1},{4,6},{5,7},{6,4},{7,5},{8,10},{9,11},{10,... | collective-permute-start | bytes 393224 | tf_op jit(solution)/shard_map/ppermute | solution.py:20
  131.9 5.8 %collective-permute-start.12 = (bf16[64,1024]{1,0:T(8,128)(2,1)S(1)}, bf16[64,1024]{1,0:T(8,128)(2,1)}, u32[]{:S(2)}, u32[]{:S(2)}) collective-permute-start(bf16[64,1024]{1,0:T(8,128)(2,1)S(1)} %fusion.3.refs_0_), channel_id=1, source_target_pairs={{0,1},{1,0},{2,3},{3,2},{4,5},{5,4},{6,7},{7,6},{8,9},{9,8},{10,11... | collective-permute-start | bytes 393224 | tf_op jit(solution)/shard_map/ppermute | solution.py:20
  143.8 1.5 collective-permute-start.19
  150.7 18.0 %collective-permute-start.20 = (bf16[64,2048]{1,0:T(8,128)(2,1)}, bf16[64,2048]{1,0:T(8,128)(2,1)S(1)}, u32[]{:S(2)}, u32[]{:S(2)}) collective-permute-start(bf16[64,2048]{1,0:T(8,128)(2,1)} %attend.5), channel_id=1, source_target_pairs={{0,3},{1,2},{2,1},{3,0},{4,7},{5,6},{6,5},{7,4},{8,11},{9,10},{10,... | collective-permute-start | bytes 786440 | tf_op jit(solution)/shard_map/ppermute | solution.py:20
  157.2 11.6 %collective-permute-start.21 = (bf16[64,2048]{1,0:T(8,128)(2,1)}, bf16[64,2048]{1,0:T(8,128)(2,1)S(1)}, u32[]{:S(2)}, u32[]{:S(2)}) collective-permute-start(bf16[64,2048]{1,0:T(8,128)(2,1)} %attend.6), channel_id=1, source_target_pairs={{0,1},{1,0},{2,3},{3,2},{4,5},{5,4},{6,7},{7,6},{8,9},{9,8},{10,11... | collective-permute-start | bytes 786440 | tf_op jit(solution)/shard_map/ppermute | solution.py:20
  163.3 8.0 %collective-permute-start.22 = (bf16[64,2048]{1,0:T(8,128)(2,1)}, bf16[64,2048]{1,0:T(8,128)(2,1)S(1)}, u32[]{:S(2)}, u32[]{:S(2)}) collective-permute-start(bf16[64,2048]{1,0:T(8,128)(2,1)} %attend.7), channel_id=1, source_target_pairs={{0,2},{1,3},{2,0},{3,1},{4,6},{5,7},{6,4},{7,5},{8,10},{9,11},{10,... | collective-permute-start | bytes 786440 | tf_op jit(solution)/shard_map/ppermute | solution.py:20
  (9 other events, 14.2 us)
